TPU v7x, 32 devices: a whole 2x2x4 slice. The times are simulated.
32 devices in a mesh: ctx: 8 (over y, x, core), head: 4 (over z).
Axes of the slice: x: 2, y: 2, z: 4, core: 2. Of those that a mesh axis runs over, the one named last changes fastest.
Arguments:
- row_query: bfloat16 [8192, 3072], P('ctx', 'head'), may hold values from -160 to 160
- row_key: bfloat16 [8192, 3072], P('ctx', 'head'), may hold values from -5 to 5
- row_value: bfloat16 [8192, 3072], P('ctx', 'head'), may hold values from -6 to 6
- row_cotangent: bfloat16 [8192, 3072], P('ctx', 'head'), may hold values from -6 to 6
- row_mask: int32 [64, 9], replicated, may hold values from 0 to 1, as said below
- col_query: bfloat16 [8192, 3072], P('ctx', 'head'), may hold values from -160 to 160
- col_key: bfloat16 [8192, 3072], P('ctx', 'head'), may hold values from -5 to 5
- col_value: bfloat16 [8192, 3072], P('ctx', 'head'), may hold values from -6 to 6
- col_cotangent: bfloat16 [8192, 3072], P('ctx', 'head'), may hold values from -6 to 6
- col_mask: int32 [64, 64], replicated, may hold values from 0 to 1, as said below
Outputs:
- row_output: bfloat16 [8192, 3072], P('ctx', 'head')
- row_dquery: bfloat16 [8192, 3072], P('ctx', 'head')
- row_dkeys: bfloat16 [8192, 3072], P('ctx', 'head')
- row_dvalues: bfloat16 [8192, 3072], P('ctx', 'head')
- col_output: bfloat16 [8192, 3072], P('ctx', 'head')
- col_dquery: bfloat16 [8192, 3072], P('ctx', 'head')
- col_dkeys: bfloat16 [8192, 3072], P('ctx', 'head')
- col_dvalues: bfloat16 [8192, 3072], P('ctx', 'head')
Inputs may be any that keep to these rules, and one draw needn't show every extreme that they name: row_mask[r, 4] = 1 for every r, row_mask[r, 3] = 1 for even r and row_mask[r, 5] = 1 for odd r; entries that point outside the grid are ignored. col_mask[r, r] = 1 for every r and col_mask[r, r - 1] = 1 for r >= 1.
All inputs are finite; a program needn't handle non-finite values.
Results may differ from a plain program's by a relative error of at most 0.022.
Values may be sent and summed in bfloat16 or wider, within the bound.
No kernel may reach another device: no remote copies, remote signals or barrier semaphores. Data moves between devices by JAX's collectives and lax.ppermute only.
A program may use at most 192 MiB of HBM per device.

v0:
```python
import jax
import jax.numpy as jnp
from jax import lax
from jax.sharding import PartitionSpec as P

HEAD_DIM = 128
GRIDC = 128
masked_score = -1e30


def padded_2(array, sides, width):
    for axis, dim in sides:
        size, length = (lax.axis_size(axis), array.shape[dim])
        up = [(i, (i + 1) % size) for i in range(size - 1)]
        down = [(j, i) for i, j in up]
        last = lax.slice_in_dim(array, length - width, length, axis=dim)
        initial = lax.slice_in_dim(array, 0, width, axis=dim)
        before = lax.ppermute(last, axis, up)
        after = lax.ppermute(initial, axis, down)
        array = jnp.concatenate([before, array, after], axis=dim)
    return array


def passed_along(block, axis, distance):
    devices = range(lax.axis_size(axis))
    route = [(i - distance, i) for i in devices if i - distance in devices]
    return lax.ppermute(block, axis, route)


def attend_block(queries, key_block, value_block, cotangent, allowed):
    scale = queries.shape[-1] ** (-0.5)
    scores = (
        jnp.einsum("bnd,bmd->bnm", queries, key_block, preferred_element_type=jnp.float32) * scale
    )
    scores = jnp.where(allowed, scores, masked_score)
    row_max = jnp.max(scores, axis=-1, keepdims=True)
    exp_terms = jnp.where(allowed, jnp.exp(scores - row_max), 0.0)
    attn_prob = exp_terms / jnp.sum(exp_terms, axis=-1, keepdims=True)
    prob_low = attn_prob.astype(jnp.bfloat16)
    output = jnp.einsum(
        "bnm,bmd->bnd", prob_low, value_block, preferred_element_type=jnp.float32
    ).astype(jnp.bfloat16)
    d_prob = jnp.einsum("bnd,bmd->bnm", cotangent, value_block, preferred_element_type=jnp.float32)
    delta_sum = jnp.sum(
        cotangent.astype(jnp.float32) * output.astype(jnp.float32), axis=-1, keepdims=True
    )
    d_scores = (attn_prob * (d_prob - delta_sum)).astype(jnp.bfloat16)
    grad_query = (
        jnp.einsum("bnm,bmd->bnd", d_scores, key_block, preferred_element_type=jnp.float32) * scale
    ).astype(jnp.bfloat16)
    grad_keys = (
        jnp.einsum("bnm,bnd->bmd", d_scores, queries, preferred_element_type=jnp.float32) * scale
    )
    grad_values = jnp.einsum(
        "bnm,bnd->bmd", prob_low, cotangent, preferred_element_type=jnp.float32
    )
    return (output, grad_query, grad_keys, grad_values)


def row_allowed(mask_rows, first, nrows, window, band, total_rows, grid_cols):
    query_rows = first + jnp.arange(nrows)[:, None]
    block_rows = query_rows + jnp.arange(window)[None, :] - band
    valid = (block_rows >= 0) & (block_rows < total_rows) & (mask_rows == 1)
    outside = (query_rows < 0) | (query_rows >= total_rows)
    valid = valid | outside
    return jnp.repeat(valid, grid_cols, axis=1)[:, None, :]


def row_pass(queries, pairs, cotangent, allowed, nrows, band, window, grid_cols):
    head_dim = HEAD_DIM
    heads = queries.shape[1] // head_dim
    head_queries = queries.reshape(nrows, grid_cols, heads, head_dim).transpose(2, 0, 1, 3)
    head_cotangent = cotangent.reshape(nrows, grid_cols, heads, head_dim).transpose(2, 0, 1, 3)
    head_pairs = pairs.reshape(2, nrows + 2 * band, grid_cols, heads, head_dim).transpose(
        3, 0, 1, 2, 4
    )

    def one_head(operands):
        head_q, head_kv, head_cot = operands
        windows = jnp.stack([head_kv[:, offset : offset + nrows] for offset in range(window)], 2)
        windows = windows.reshape(2, nrows, window * grid_cols, head_dim)
        output, grad_query, grad_keys, grad_values = attend_block(
            head_q, windows[0], windows[1], head_cot, allowed
        )
        grads = jnp.stack([grad_keys, grad_values]).reshape(2, nrows, window, grid_cols, head_dim)
        accum = jnp.zeros((2, nrows + 2 * band, grid_cols, head_dim), jnp.float32)
        for offset in range(window):
            accum = accum.at[:, offset : offset + nrows].add(grads[:, :, offset])
        return (output, grad_query, accum)

    return lax.map(one_head, (head_queries, head_pairs, head_cotangent))


def body(
    row_query,
    row_key,
    row_value,
    row_cotangent,
    row_mask,
    col_query,
    col_key,
    col_value,
    col_cotangent,
    col_mask,
):
    head_dim = HEAD_DIM
    grid_cols = GRIDC
    tokens = row_query.shape[0]
    rows_here = tokens // grid_cols
    window = row_mask.shape[1]
    band = (window - 1) // 2
    row_feat = row_query.shape[1]
    first_row = lax.axis_index("ctx") * rows_here
    total_rows = rows_here * lax.axis_size("ctx")
    key_value = jnp.stack([row_key, row_value])
    padded = padded_2(key_value, (("ctx", 1),), band * grid_cols)
    mask_rows = lax.dynamic_slice_in_dim(row_mask, first_row, rows_here, 0)
    allowed_rows = row_allowed(mask_rows, first_row, rows_here, window, band, total_rows, grid_cols)
    outputs, grad_queries, accums = row_pass(
        row_query, padded, row_cotangent, allowed_rows, rows_here, band, window, grid_cols
    )
    lower_rim = accums[:, :, :band]
    upper_rim = accums[:, :, band + rows_here :]
    own_grads = accums[:, :, band : band + rows_here]
    from_next = passed_along(lower_rim.astype(jnp.bfloat16), "ctx", -1).astype(lower_rim.dtype)
    from_prev = passed_along(upper_rim.astype(jnp.bfloat16), "ctx", 1).astype(upper_rim.dtype)
    own_grads = own_grads.at[:, :, rows_here - band :].add(from_next)
    own_grads = own_grads.at[:, :, :band].add(from_prev)
    own_grads = own_grads.transpose(1, 2, 3, 0, 4).reshape(2, tokens, row_feat).astype(jnp.bfloat16)
    row_output = outputs.transpose(1, 2, 0, 3).reshape(tokens, row_feat)
    row_dquery = grad_queries.transpose(1, 2, 0, 3).reshape(tokens, row_feat)
    row_dkeys = own_grads[0]
    row_dvalues = own_grads[1]
    col_feat = col_query.shape[1]
    n_ctx = lax.axis_size("ctx")
    grid_rows = rows_here * n_ctx
    stacked = jnp.stack([col_query, col_key, col_value, col_cotangent]).reshape(
        4, rows_here, grid_cols, col_feat
    )
    moved = lax.all_to_all(stacked, "ctx", split_axis=2, concat_axis=1, tiled=True)
    cols_here = moved.shape[2]
    all_heads = moved.shape[3] // head_dim
    batched = moved.reshape(4, grid_rows, cols_here, all_heads, head_dim).transpose(0, 2, 3, 1, 4)
    batched = batched.reshape(4, cols_here * all_heads, grid_rows, head_dim)
    allowed_cols = (col_mask == 1)[None]
    output, grad_query, grad_keys, grad_values = attend_block(
        batched[0], batched[1], batched[2], batched[3], allowed_cols
    )
    results = jnp.stack(
        [output, grad_query, grad_keys.astype(jnp.bfloat16), grad_values.astype(jnp.bfloat16)]
    )
    results = results.reshape(4, cols_here, all_heads, grid_rows, head_dim).transpose(0, 3, 1, 2, 4)
    results = results.reshape(4, grid_rows, cols_here, all_heads * head_dim)
    returned = lax.all_to_all(results, "ctx", split_axis=1, concat_axis=2, tiled=True)
    returned = returned.reshape(4, tokens, col_feat)
    return (
        row_output,
        row_dquery,
        row_dkeys,
        row_dvalues,
        returned[0],
        returned[1],
        returned[2],
        returned[3],
    )


def solution(mesh):
    return jax.shard_map(
        body,
        mesh=mesh,
        in_specs=(
            P("ctx", "head"),
            P("ctx", "head"),
            P("ctx", "head"),
            P("ctx", "head"),
            P(),
            P("ctx", "head"),
            P("ctx", "head"),
            P("ctx", "head"),
            P("ctx", "head"),
            P(),
        ),
        out_specs=(
            P("ctx", "head"),
            P("ctx", "head"),
            P("ctx", "head"),
            P("ctx", "head"),
            P("ctx", "head"),
            P("ctx", "head"),
            P("ctx", "head"),
            P("ctx", "head"),
        ),
        check_vma=False,
    )
```

profile of v0, /device:TPU:11, one launch (start us, length us, event | category | flops | bytes accessed | tf_op | source)
XLA Modules:
  0.0 450.1 jit_solution(2632079442033608553)
XLA Ops:
  4.4 6.3 %copy.209 = bf16[4,8,128,768]{3,1,0,2:T(8,128)(2,1)} copy(bf16[4,8,128,768]{3,2,1,0:T(8,128)(2,1)S(1)} %pad_maximum_fusion.2) | data formatting | bytes 12582912 | tf_op jit(solution)/shard_map/stack | solution.py:137
  10.6 5.8 %all-to-all-start = ((bf16[4,8,128,768]{3,1,0,2:T(8,128)(2,1)}), bf16[4,8,128,768]{3,1,0,2:T(8,128)(2,1)}, u32[]{:S(2)}, u32[]{:S(2)}) async-start(bf16[4,8,128,768]{3,1,0,2:T(8,128)(2,1)} %copy.209), calls=%async_computation | async-start | bytes 12582912 | tf_op jit(solution)/shard_map/all_to_all | solution.py:140
  36.3 83.7 %collective-permute-done.1 = bf16[2,512,768]{2,1,0:T(8,128)(2,1)} collective-permute-done((bf16[2,512,768]{2,1,0:T(8,128)(2,1)}, bf16[2,512,768]{2,1,0:T(8,128)(2,1)}, u32[]{:S(2)}, u32[]{:S(2)}) %collective-permute-start.1) | collective-permute-done | bytes 1572896 | tf_op jit(solution)/shard_map/ppermute | solution.py:19
  120.0 5.1 %pad_maximum_fusion.1 = bf16[2,2048,768]{2,1,0:T(8,128)(2,1)} fusion(bf16[2,512,768]{2,1,0:T(8,128)(2,1)} %collective-permute-done.1, bf16[1,1024,768]{2,1,0:T(8,128)(2,1)S(1)} %bitcast.375, bf16[1,1024,768]{2,1,0:T(8,128)(2,1)S(1)} %bitcast.373, bf16[2,512,768]{2,1,0:T(8,128)(2,1)} %collective-permute-done), kind=kLoop, calls=%fused_computation.102 | loop fusion | flops 25165824 | bytes 12582912 | tf_op jit(solution)/shard_map/concatenate | solution.py:20
  125.2 8.7 %copy.198 = bf16[2,2048,768]{1,2,0:T(8,128)(2,1)} copy(bf16[2,2048,768]{2,1,0:T(8,128)(2,1)} %pad_maximum_fusion.1) | data formatting | bytes 12582912 | tf_op jit(solution)/shard_map/concatenate | solution.py:20
  133.8 7.7 %copy.264 = bf16[192,8,16,128]{3,2,1,0:T(8,128)(2,1)} copy(bf16[192,8,16,128]{3,1,2,0:T(8,128)(2,1)} %bitcast.366) | data formatting | bytes 12582912
  141.6 10.6 %copy.211 = bf16[4,8,8,16,768]{4,3,2,1,0:T(8,128)(2,1)} copy(bf16[4,8,8,16,768]{4,2,0,3,1:T(8,128)(2,1)} %bitcast.14) | data formatting | bytes 12582912 | tf_op jit(solution)/shard_map/all_to_all | solution.py:140
  152.2 13.6 %reshape.576 = bf16[4,64,16,6,128]{4,3,2,1,0:T(8,128)(2,1)} reshape(bf16[4,8,8,16,768]{4,3,2,1,0:T(8,128)(2,1)} %copy.211) | data formatting | bytes 12582912 | tf_op jit(solution)/shard_map/reshape | solution.py:143
  165.8 5.8 %fusion.85 = (bf16[1,16,6,64,128]{4,2,1,3,0:T(8,128)(2,1)S(1)}, bf16[1,16,6,64,128]{4,2,1,3,0:T(8,128)(2,1)S(1)}, bf16[1,16,6,64,128]{4,2,1,3,0:T(8,128)(2,1)S(1)}, bf16[1,16,6,64,128]{4,2,1,3,0:T(8,128)(2,1)S(1)}) fusion(bf16[4,16,6,64,128]{4,2,1,3,0:T(8,128)(2,1)} %bitcast.364), kind=kLoop, calls=%fused_computation.144 | loop fusion | bytes 12582912 | tf_op jit(solution)/shard_map/slice | solution.py:147
  193.7 4.4 maximum_bitcast_fusion
  198.1 13.8 %reshape.577 = bf16[4,64,16,768]{3,2,1,0:T(8,128)(2,1)} reshape(bf16[4,64,16,6,128]{4,3,2,1,0:T(8,128)(2,1)} %maximum_bitcast_fusion) | data formatting | bytes 12582912 | tf_op jit(solution)/shard_map/reshape | solution.py:153
  211.9 6.3 %copy.223 = bf16[4,64,16,768]{3,2,0,1:T(8,128)(2,1)} copy(bf16[4,64,16,768]{3,2,1,0:T(8,128)(2,1)} %reshape.577) | data formatting | bytes 12582912 | tf_op jit(solution)/shard_map/reshape | solution.py:153
  218.2 4.7 %all-to-all-start.1 = ((bf16[4,64,16,768]{3,2,0,1:T(8,128)(2,1)}), bf16[4,64,16,768]{3,2,0,1:T(8,128)(2,1)}, u32[]{:S(2)}, u32[]{:S(2)}) async-start(bf16[4,64,16,768]{3,2,0,1:T(8,128)(2,1)} %copy.223), calls=%async_computation.1 | async-start | bytes 12582912 | tf_op jit(solution)/shard_map/all_to_all | solution.py:154
  222.9 160.0 %while.29 = (s32[]{:T(128)}, bf16[6,8,128,128]{2,3,1,0:T(8,128)(2,1)}, bf16[6,8,128,128]{3,2,1,0:T(8,128)(2,1)}, f32[6,2,16,128,128]{4,3,2,1,0:T(8,128)}, bf16[6...) while((s32[]{:T(128)}, ...), condition=%wide.region_4.5_spmd.clone, body=%wide.region_0.4_spmd.clone.sunk | while | flops 1831469184 | bytes 216832256 | solution.py:91
  229.8 5.7 %fusion.166 = (f32[8,128]{1,0:T(8,128)S(1)}, f32[8,128,1152]{2,1,0:T(8,128)}) fusion(bf16[8,1152,128]{2,1,0:T(8,128)(2,1)} %bitcast.362, pred[8,1152]{1,0:T(8,128)(4,1)S(1)} %broadcast_bitcast_fusion.2, bf16[1,8,128,128]{3,2,1,0:T(8,128)(2,1)S(1)} %copy.288), kind=kOutput, calls=%fused_computation.143.clone.1 | convolution fusion | flops 307889280 | bytes 7353344 | tf_op jit(solution)/shard_map/while/body/eval_jaxpr/sub | solution.py:37
  256.4 5.7 %fusion.166 = (f32[8,128]{1,0:T(8,128)S(1)}, f32[8,128,1152]{2,1,0:T(8,128)}) fusion(bf16[8,1152,128]{2,1,0:T(8,128)(2,1)} %bitcast.362, pred[8,1152]{1,0:T(8,128)(4,1)S(1)} %broadcast_bitcast_fusion.2, bf16[1,8,128,128]{3,2,1,0:T(8,128)(2,1)S(1)} %copy.288), kind=kOutput, calls=%fused_computation.143.clone.1 | convolution fusion | flops 307889280 | bytes 7353344 | tf_op jit(solution)/shard_map/while/body/eval_jaxpr/sub | solution.py:37
  283.0 5.7 %fusion.166 = (f32[8,128]{1,0:T(8,128)S(1)}, f32[8,128,1152]{2,1,0:T(8,128)}) fusion(bf16[8,1152,128]{2,1,0:T(8,128)(2,1)} %bitcast.362, pred[8,1152]{1,0:T(8,128)(4,1)S(1)} %broadcast_bitcast_fusion.2, bf16[1,8,128,128]{3,2,1,0:T(8,128)(2,1)S(1)} %copy.288), kind=kOutput, calls=%fused_computation.143.clone.1 | convolution fusion | flops 307889280 | bytes 7353344 | tf_op jit(solution)/shard_map/while/body/eval_jaxpr/sub | solution.py:37
  309.7 5.7 %fusion.166 = (f32[8,128]{1,0:T(8,128)S(1)}, f32[8,128,1152]{2,1,0:T(8,128)}) fusion(bf16[8,1152,128]{2,1,0:T(8,128)(2,1)} %bitcast.362, pred[8,1152]{1,0:T(8,128)(4,1)S(1)} %broadcast_bitcast_fusion.2, bf16[1,8,128,128]{3,2,1,0:T(8,128)(2,1)S(1)} %copy.288), kind=kOutput, calls=%fused_computation.143.clone.1 | convolution fusion | flops 307889280 | bytes 7353344 | tf_op jit(solution)/shard_map/while/body/eval_jaxpr/sub | solution.py:37
  336.3 5.7 %fusion.166 = (f32[8,128]{1,0:T(8,128)S(1)}, f32[8,128,1152]{2,1,0:T(8,128)}) fusion(bf16[8,1152,128]{2,1,0:T(8,128)(2,1)} %bitcast.362, pred[8,1152]{1,0:T(8,128)(4,1)S(1)} %broadcast_bitcast_fusion.2, bf16[1,8,128,128]{3,2,1,0:T(8,128)(2,1)S(1)} %copy.288), kind=kOutput, calls=%fused_computation.143.clone.1 | convolution fusion | flops 307889280 | bytes 7353344 | tf_op jit(solution)/shard_map/while/body/eval_jaxpr/sub | solution.py:37
  363.0 5.7 %fusion.166 = (f32[8,128]{1,0:T(8,128)S(1)}, f32[8,128,1152]{2,1,0:T(8,128)}) fusion(bf16[8,1152,128]{2,1,0:T(8,128)(2,1)} %bitcast.362, pred[8,1152]{1,0:T(8,128)(4,1)S(1)} %broadcast_bitcast_fusion.2, bf16[1,8,128,128]{3,2,1,0:T(8,128)(2,1)S(1)} %copy.288), kind=kOutput, calls=%fused_computation.143.clone.1 | convolution fusion | flops 307889280 | bytes 7353344 | tf_op jit(solution)/shard_map/while/body/eval_jaxpr/sub | solution.py:37
  383.0 6.2 %convert.4 = bf16[6,2,16,128,128]{4,3,2,1,0:T(8,128)(2,1)S(1)} convert(f32[6,2,16,128,128]{4,3,2,1,0:T(8,128)} %get-tuple-element.300) | non-fusion elementwise | flops 3145728 | bytes 18874368 | tf_op jit(solution)/shard_map/convert.1
  393.0 4.7 %collective-permute-start.3 = (bf16[6,2,4,128,128]{4,3,2,1,0:T(8,128)(2,1)}, bf16[6,2,4,128,128]{4,3,2,1,0:T(8,128)(2,1)}, u32[]{:S(2)}, u32[]{:S(2)}) collective-permute-start(bf16[6,2,4,128,128]{4,3,2,1,0:T(8,128)(2,1)} %get-tuple-element.424), channel_id=1, source_target_pairs={{0,4},{4,8},{8,12},{12,16},{16,20},{20,24},{24,28},{1,5},{5,9},{9,... | collective-permute-start | bytes 4718600 | tf_op jit(solution)/shard_map/ppermute | solution.py:27
  397.7 6.3 %slice.552 = f32[6,2,8,128,128]{4,3,2,1,0:T(8,128)} slice(f32[6,2,16,128,128]{4,3,2,1,0:T(8,128)} %get-tuple-element.300), slice={[0:6], [0:2], [4:12], [0:128], [0:128]} | slice | bytes 12582912 | tf_op jit(solution)/shard_map/slice | solution.py:124
  413.3 16.9 %collective-permute-done.2 = bf16[6,2,4,128,128]{4,3,2,1,0:T(8,128)(2,1)} collective-permute-done((bf16[6,2,4,128,128]{4,3,2,1,0:T(8,128)(2,1)}, bf16[6,2,4,128,128]{4,3,2,1,0:T(8,128)(2,1)}, u32[]{:S(2)}, u32[]{:S(2)}) %collective-permute-start.2) | collective-permute-done | bytes 1572896 | tf_op jit(solution)/shard_map/ppermute | solution.py:27
  (298 shorter events, 202.7 us)
Async XLA Ops:
  10.6 5.8 %copy-start.3 = (bf16[1024,768]{1,0:T(8,128)(2,1)S(1)}, bf16[1024,768]{1,0:T(8,128)(2,1)}, u32[]{:S(2)}) copy-start(bf16[1024,768]{1,0:T(8,128)(2,1)} %param.35) | copy-start | bytes 4718596
  10.6 5.8 %copy-start.4 = (bf16[1024,768]{1,0:T(8,128)(2,1)S(1)}, bf16[1024,768]{1,0:T(8,128)(2,1)}, u32[]{:S(2)}) copy-start(bf16[1024,768]{1,0:T(8,128)(2,1)} %param.36) | copy-start | bytes 4718596
  10.6 130.9 %all-to-all-start = ((bf16[4,8,128,768]{3,1,0,2:T(8,128)(2,1)}), bf16[4,8,128,768]{3,1,0,2:T(8,128)(2,1)}, u32[]{:S(2)}, u32[]{:S(2)}) async-start(bf16[4,8,128,768]{3,1,0,2:T(8,128)(2,1)} %copy.209), calls=%async_computation | async-start | bytes 12582912 | tf_op jit(solution)/shard_map/all_to_all | solution.py:140
  18.2 101.8 %collective-permute-start.1 = (bf16[2,512,768]{2,1,0:T(8,128)(2,1)}, bf16[2,512,768]{2,1,0:T(8,128)(2,1)}, u32[]{:S(2)}, u32[]{:S(2)}) collective-permute-start(bf16[2,512,768]{2,1,0:T(8,128)(2,1)} %get-tuple-element.429), channel_id=1, source_target_pairs={{4,0},{8,4},{12,8},{16,12},{20,16},{24,20},{28,24},{5,1},{9,5},{13... | collective-permute-start | bytes 4718600 | tf_op jit(solution)/shard_map/ppermute | solution.py:19
  20.5 99.5 %collective-permute-start = (bf16[2,512,768]{2,1,0:T(8,128)(2,1)}, bf16[2,512,768]{2,1,0:T(8,128)(2,1)}, u32[]{:S(2)}, u32[]{:S(2)}) collective-permute-start(bf16[2,512,768]{2,1,0:T(8,128)(2,1)} %get-tuple-element.428), channel_id=1, source_target_pairs={{0,4},{4,8},{8,12},{12,16},{16,20},{20,24},{24,28},{1,5},{5,9},{9,... | collective-permute-start | bytes 4718600 | tf_op jit(solution)/shard_map/ppermute | solution.py:18
  33.1 3.0 copy-start.8
  33.1 3.2 copy-start.9
  181.2 3.1 copy-start.6
  181.2 3.3 copy-start.7
  181.2 4.3 copy-start.10
  218.2 222.7 %all-to-all-start.1 = ((bf16[4,64,16,768]{3,2,0,1:T(8,128)(2,1)}), bf16[4,64,16,768]{3,2,0,1:T(8,128)(2,1)}, u32[]{:S(2)}, u32[]{:S(2)}) async-start(bf16[4,64,16,768]{3,2,0,1:T(8,128)(2,1)} %copy.223), calls=%async_computation.1 | async-start | bytes 12582912 | tf_op jit(solution)/shard_map/all_to_all | solution.py:154
  238.3 2.4 copy-start
  240.8 1.7 copy-start.1
  265.0 2.4 copy-start
  267.4 1.7 copy-start.1
  291.6 2.4 copy-start
  318.2 2.4 copy-start
  320.7 1.7 copy-start.1
  344.9 2.4 copy-start
  371.5 2.4 copy-start
  391.0 39.2 %collective-permute-start.2 = (bf16[6,2,4,128,128]{4,3,2,1,0:T(8,128)(2,1)}, bf16[6,2,4,128,128]{4,3,2,1,0:T(8,128)(2,1)}, u32[]{:S(2)}, u32[]{:S(2)}) collective-permute-start(bf16[6,2,4,128,128]{4,3,2,1,0:T(8,128)(2,1)} %get-tuple-element.425), channel_id=1, source_target_pairs={{4,0},{8,4},{12,8},{16,12},{20,16},{24,20},{28,24},{5,1},{9,5},{13... | collective-permute-start | bytes 4718600 | tf_op jit(solution)/shard_map/ppermute | solution.py:27
  393.0 11.0 %copy-start.5 = (bf16[6,8,128,128]{3,2,1,0:T(8,128)(2,1)S(1)}, bf16[6,8,128,128]{3,2,1,0:T(8,128)(2,1)}, u32[]{:S(2)}) copy-start(bf16[6,8,128,128]{3,2,1,0:T(8,128)(2,1)} %get-tuple-element.299) | copy-start | bytes 4718596
  393.0 40.0 %collective-permute-start.3 = (bf16[6,2,4,128,128]{4,3,2,1,0:T(8,128)(2,1)}, bf16[6,2,4,128,128]{4,3,2,1,0:T(8,128)(2,1)}, u32[]{:S(2)}, u32[]{:S(2)}) collective-permute-start(bf16[6,2,4,128,128]{4,3,2,1,0:T(8,128)(2,1)} %get-tuple-element.424), channel_id=1, source_target_pairs={{0,4},{4,8},{8,12},{12,16},{16,20},{20,24},{24,28},{1,5},{5,9},{9,... | collective-permute-start | bytes 4718600 | tf_op jit(solution)/shard_map/ppermute | solution.py:27
  409.0 21.2 %copy-start.2 = (f32[6,2,8,128,128]{4,3,2,1,0:T(8,128)S(1)}, f32[6,2,8,128,128]{4,3,2,1,0:T(8,128)}, u32[]{:S(2)}) copy-start(f32[6,2,8,128,128]{4,3,2,1,0:T(8,128)} %slice.552) | copy-start | bytes 18874372
  (3 other events, 5.0 us)
where the time goes:
time: 457 us; the launch traced here: 450 us
  local copies, waits for them, and re-layouts  185 us (40%)
  waiting for transfers between devices  101 us (22%)
  matrix products  82.3 us (18%)
  other arithmetic  56.6 us (12%)
  starting transfers between devices  23.7 us (5%)
    ppermute x1, waiting for transfers between devices, padded_2(): after = lax.ppermute(initial, axis, down)  83.7 us
    sub x7, matrix products, attend_block(): exp_terms = jnp.where(allowed, jnp.exp(scores - row_max), 0.0)  37.6 us
    unnamed x29, local copies, waits for them, and re-layouts  34.3 us
    dynamic_slice x24, local copies, waits for them, and re-layouts, row_pass(): return lax.map(one_head, (head_queries, head_pairs, head_cotangent))  22.1 us
    reshape x2, local copies, waits for them, and re-layouts, body(): results = results.reshape(4, grid_rows, cols_here, all_heads * head_dim)  20.1 us
    convert_element_type x6, other arithmetic, attend_block(): prob_low = attn_prob.astype(jnp.bfloat16)  17.1 us
    ppermute x2, waiting for transfers between devices, passed_along(): return lax.ppermute(block, axis, route)  16.9 us
    slice x6, local copies, waits for them, and re-layouts, one_head(): windows[1]  14.1 us
  transfers between devices with their start and end apart: 6, of which 2 were waited for; matrix products, arithmetic and copies ran while one was open for 49% of the time, Pallas kernels for 0%

commit v1 on v0

--- a/solution.py
+++ b/solution.py
@@ -137,7 +137,15 @@
     stacked = jnp.stack([col_query, col_key, col_value, col_cotangent]).reshape(
         4, rows_here, grid_cols, col_feat
     )
-    moved = lax.all_to_all(stacked, "ctx", split_axis=2, concat_axis=1, tiled=True)
+    ways, here = (lax.axis_size("ctx"), lax.axis_index("ctx"))
+    width_2 = stacked.shape[2] // ways
+    turned = jnp.roll(stacked, -here * width_2, axis=2)
+    got = [lax.slice_in_dim(turned, 0, width_2, axis=2)]
+    for far in range(1, ways):
+        sent = lax.slice_in_dim(turned, far * width_2, (far + 1) * width_2, axis=2)
+        got.append(lax.ppermute(sent, "ctx", [(d, (d + far) % ways) for d in range(ways)]))
+    line = jnp.concatenate(got[::-1], axis=1)
+    moved = jnp.roll(line, (here + 1) * got[0].shape[1], axis=1)
     cols_here = moved.shape[2]
     all_heads = moved.shape[3] // head_dim
     batched = moved.reshape(4, grid_rows, cols_here, all_heads, head_dim).transpose(0, 2, 3, 1, 4)

time: 457 us -> 430 us (0.941)
  waiting for transfers between devices: 101 us -> 37.4 us
  starting transfers between devices: 23.7 us -> 51.3 us
    ppermute x1, waiting for transfers between devices: 83.7 us -> 0.01 us  [padded_2(): after = lax.ppermute(initial, axis, down)]
    ppermute x0 -> x7, waiting for transfers between devices: none -> 22 us  [body(): lax.ppermute(sent, 'ctx', [(d, (d + far) % ways) for d in range(ways)])]
    ppermute x0 -> x7, starting transfers between devices: none -> 20 us  [body(): lax.ppermute(sent, 'ctx', [(d, (d + far) % ways) for d in range(ways)])]
    unnamed x29 -> x54, local copies, waits for them, and re-layouts: 34.3 us -> 47 us
    ppermute x1, starting transfers between devices: 4.37 us -> 16.6 us  [padded_2(): before = lax.ppermute(last, axis, up)]
    all_to_all x1 -> x0, local copies, waits for them, and re-layouts: 10.6 us -> none  [body(): lax.all_to_all(stacked, 'ctx', split_axis=2, concat_axis=1, tiled=True)]
    concatenate x0 -> x1, other arithmetic: none -> 6.61 us  [body(): turned = jnp.roll(stacked, -here * width_2, axis=2)]
    another operation x1 -> x0, local copies, waits for them, and re-layouts: 6.25 us -> none  [body(): jnp.stack([col_query, col_key, col_value, col_cotangent])]
  transfers between devices with their start and end apart: 6 -> 12, of which waited for: 2 -> 3; matrix products, arithmetic and copies ran while one was open for 49% -> 73% of each run, Pallas kernels for 0% -> 0%
where the time goes in v1:
time: 430 us; the launch traced here: 421 us
  local copies, waits for them, and re-layouts  185 us (43%)
  matrix products  83.9 us (20%)
  other arithmetic  60.4 us (14%)
  starting transfers between devices  51.3 us (12%)
  waiting for transfers between devices  37.4 us (9%)
    unnamed x54, local copies, waits for them, and re-layouts  47 us
    sub x7, matrix products, attend_block(): exp_terms = jnp.where(allowed, jnp.exp(scores - row_max), 0.0)  38.8 us
    dynamic_slice x24, local copies, waits for them, and re-layouts, row_pass(): return lax.map(one_head, (head_queries, head_pairs, head_cotangent))  22.1 us
    ppermute x7, waiting for transfers between devices, body(): lax.ppermute(sent, 'ctx', [(d, (d + far) % ways) for d in range(ways)])  22 us
    reshape x2, local copies, waits for them, and re-layouts, body(): results = results.reshape(4, grid_rows, cols_here, all_heads * head_dim)  20.1 us
    ppermute x7, starting transfers between devices, body(): lax.ppermute(sent, 'ctx', [(d, (d + far) % ways) for d in range(ways)])  20 us
    convert_element_type x6, other arithmetic, attend_block(): prob_low = attn_prob.astype(jnp.bfloat16)  18 us
    ppermute x1, starting transfers between devices, padded_2(): before = lax.ppermute(last, axis, up)  16.6 us
  transfers between devices with their start and end apart: 12, of which 3 were waited for; matrix products, arithmetic and copies ran while one was open for 73% of the time, Pallas kernels for 0%

profile of v1, /device:TPU:11, one launch (start us, length us, event | category | flops | bytes accessed | tf_op | source)
XLA Modules:
  0.0 421.5 jit_solution(4123849400604060426)
XLA Ops:
  0.7 6.6 %fusion.68 = bf16[4,8,128,768]{3,2,1,0:T(8,128)(2,1)S(1)} fusion(s32[]{:T(128)S(6)} %select_n.50, bf16[1,8,128,768]{3,2,1,0:T(8,128)(2,1)} %bitcast.385, bf16[1,8,128,768]{3,2,1,0:T(8,128)(2,1)} %bitcast.386, bf16[1,8,128,768]{3,2,1,0:T(8,128)(2,1)} %bitcast.387, bf16[1,8,128,768]{3,2,1,0:T(8,128)(2,1)} %bitcast.388), kind=kLoop, calls=%fused_computation.113 | loop fusion | flops 50331648 | bytes 12582916 | tf_op jit(solution)/shard_map/jit(_roll_dynamic)/concatenate | solution.py:142
  24.6 8.4 %collective-permute-done.4 = bf16[4,8,16,768]{3,2,1,0:T(8,128)(2,1)} collective-permute-done((bf16[4,8,16,768]{3,2,1,0:T(8,128)(2,1)}, bf16[4,8,16,768]{3,2,1,0:T(8,128)(2,1)}, u32[]{:S(2)}, u32[]{:S(2)}) %collective-permute-start.4) | collective-permute-done | bytes 786464 | tf_op jit(solution)/shard_map/ppermute | solution.py:146
  35.0 15.3 %collective-permute-start.10 = (bf16[4,8,16,768]{3,2,1,0:T(8,128)(2,1)S(1)}, bf16[4,8,16,768]{3,2,1,0:T(8,128)(2,1)S(1)}, u32[]{:S(2)}, u32[]{:S(2)}) collective-permute-start(bf16[4,8,16,768]{3,2,1,0:T(8,128)(2,1)S(1)} %copy-done.11), channel_id=1, source_target_pairs={{0,4},{4,8},{8,12},{12,16},{16,20},{20,24},{24,28},{28,0},{1,5},{5... | collective-permute-start | bytes 2359304 | tf_op jit(solution)/shard_map/ppermute | solution.py:146
  52.7 13.5 %collective-permute-done.6 = bf16[4,8,16,768]{3,2,1,0:T(8,128)(2,1)} collective-permute-done((bf16[4,8,16,768]{3,2,1,0:T(8,128)(2,1)}, bf16[4,8,16,768]{3,2,1,0:T(8,128)(2,1)}, u32[]{:S(2)}, u32[]{:S(2)}) %collective-permute-start.6) | collective-permute-done | bytes 786464 | tf_op jit(solution)/shard_map/ppermute | solution.py:146
  69.3 16.6 %collective-permute-start = (bf16[2,512,768]{2,1,0:T(8,128)(2,1)}, bf16[2,512,768]{2,1,0:T(8,128)(2,1)}, u32[]{:S(2)}, u32[]{:S(2)}) collective-permute-start(bf16[2,512,768]{2,1,0:T(8,128)(2,1)} %get-tuple-element.419), channel_id=1, source_target_pairs={{0,4},{4,8},{8,12},{12,16},{16,20},{20,24},{24,28},{1,5},{5,9},{9,... | collective-permute-start | bytes 4718600 | tf_op jit(solution)/shard_map/ppermute | solution.py:18
  100.2 13.7 %reshape.575 = bf16[4,64,16,6,128]{4,3,2,1,0:T(8,128)(2,1)} reshape(bf16[4,64,16,768]{3,2,1,0:T(8,128)(2,1)} %constant_dynamic-slice_fusion.3) | data formatting | bytes 12582912 | tf_op jit(solution)/shard_map/reshape | solution.py:151
  113.9 5.5 %fusion.92 = (bf16[1,16,6,64,128]{4,2,1,3,0:T(8,128)(2,1)S(1)}, bf16[1,16,6,64,128]{4,2,1,3,0:T(8,128)(2,1)S(1)}, bf16[1,16,6,64,128]{4,2,1,3,0:T(8,128)(2,1)S(1)}, bf16[1,16,6,64,128]{4,2,1,3,0:T(8,128)(2,1)S(1)}) fusion(bf16[4,16,6,64,128]{4,2,1,3,0:T(8,128)(2,1)} %bitcast.363), kind=kLoop, calls=%fused_computation.175 | loop fusion | bytes 12582912 | tf_op jit(solution)/shard_map/slice | solution.py:155
  128.1 5.0 %fusion.97 = (f32[96,64]{1,0:T(8,128)S(1)}, f32[96,64,64]{1,2,0:T(8,128)}) fusion(pred[64,64]{0,1:T(8,128)(4,1)S(1)} %copy.157, bf16[96,64,128]{2,1,0:T(8,128)(2,1)} %bitcast.377, bf16[96,64,128]{2,1,0:T(8,128)(2,1)} %bitcast.375), kind=kOutput, calls=%fused_computation.180 | convolution fusion | flops 102629440 | bytes 4747264 | tf_op jit(solution)/shard_map/sub | solution.py:37
  150.7 13.8 %reshape.576 = bf16[4,64,16,768]{3,2,1,0:T(8,128)(2,1)} reshape(bf16[4,64,16,6,128]{4,3,2,1,0:T(8,128)(2,1)} %maximum_bitcast_fusion) | data formatting | bytes 12582912 | tf_op jit(solution)/shard_map/reshape | solution.py:161
  164.5 6.3 %copy.169 = bf16[4,64,16,768]{3,2,0,1:T(8,128)(2,1)} copy(bf16[4,64,16,768]{3,2,1,0:T(8,128)(2,1)} %reshape.576) | data formatting | bytes 12582912 | tf_op jit(solution)/shard_map/reshape | solution.py:161
  170.8 6.2 %all-to-all-start = ((bf16[4,64,16,768]{3,2,0,1:T(8,128)(2,1)}), bf16[4,64,16,768]{3,2,0,1:T(8,128)(2,1)}, u32[]{:S(2)}, u32[]{:S(2)}) async-start(bf16[4,64,16,768]{3,2,0,1:T(8,128)(2,1)} %copy.169), calls=%async_computation | async-start | bytes 12582912 | tf_op jit(solution)/shard_map/all_to_all | solution.py:162
  177.0 5.0 %pad_maximum_fusion.1 = bf16[2,2048,768]{2,1,0:T(8,128)(2,1)} fusion(bf16[2,512,768]{2,1,0:T(8,128)(2,1)} %collective-permute-done.1, bf16[1,1024,768]{2,1,0:T(8,128)(2,1)S(1)} %bitcast.374, bf16[1,1024,768]{2,1,0:T(8,128)(2,1)S(1)} %bitcast.372, bf16[2,512,768]{2,1,0:T(8,128)(2,1)} %collective-permute-done), kind=kLoop, calls=%fused_computation.117 | loop fusion | flops 25165824 | bytes 12582912 | tf_op jit(solution)/shard_map/concatenate | solution.py:20
  182.0 8.7 %copy.147 = bf16[2,2048,768]{1,2,0:T(8,128)(2,1)} copy(bf16[2,2048,768]{2,1,0:T(8,128)(2,1)} %pad_maximum_fusion.1) | data formatting | bytes 12582912 | tf_op jit(solution)/shard_map/concatenate | solution.py:20
  190.7 7.8 %copy.209 = bf16[192,8,16,128]{3,2,1,0:T(8,128)(2,1)} copy(bf16[192,8,16,128]{3,1,2,0:T(8,128)(2,1)} %bitcast.365) | data formatting | bytes 12582912
  198.6 157.4 %while.29 = (s32[]{:T(128)}, bf16[6,8,128,128]{2,3,1,0:T(8,128)(2,1)}, bf16[6,8,128,128]{3,2,1,0:T(8,128)(2,1)}, f32[6,2,16,128,128]{4,3,2,1,0:T(8,128)}, bf16[6...) while((s32[]{:T(128)}, ...), condition=%wide.region_4.5_spmd.clone, body=%wide.region_0.4_spmd.clone.sunk | while | flops 1831469184 | bytes 212113696 | solution.py:91
  205.8 5.6 %fusion.174 = (f32[8,128]{1,0:T(8,128)S(1)}, f32[8,128,1152]{2,1,0:T(8,128)}) fusion(bf16[8,1152,128]{2,1,0:T(8,128)(2,1)} %bitcast.361, pred[8,1152]{1,0:T(8,128)(4,1)S(1)} %broadcast_bitcast_fusion.2, bf16[1,8,128,128]{3,2,1,0:T(8,128)(2,1)S(1)} %copy.233), kind=kOutput, calls=%fused_computation.174.clone.1 | convolution fusion | flops 307889280 | bytes 7353344 | tf_op jit(solution)/shard_map/while/body/eval_jaxpr/sub | solution.py:37
  231.9 5.6 %fusion.174 = (f32[8,128]{1,0:T(8,128)S(1)}, f32[8,128,1152]{2,1,0:T(8,128)}) fusion(bf16[8,1152,128]{2,1,0:T(8,128)(2,1)} %bitcast.361, pred[8,1152]{1,0:T(8,128)(4,1)S(1)} %broadcast_bitcast_fusion.2, bf16[1,8,128,128]{3,2,1,0:T(8,128)(2,1)S(1)} %copy.233), kind=kOutput, calls=%fused_computation.174.clone.1 | convolution fusion | flops 307889280 | bytes 7353344 | tf_op jit(solution)/shard_map/while/body/eval_jaxpr/sub | solution.py:37
  258.0 5.6 %fusion.174 = (f32[8,128]{1,0:T(8,128)S(1)}, f32[8,128,1152]{2,1,0:T(8,128)}) fusion(bf16[8,1152,128]{2,1,0:T(8,128)(2,1)} %bitcast.361, pred[8,1152]{1,0:T(8,128)(4,1)S(1)} %broadcast_bitcast_fusion.2, bf16[1,8,128,128]{3,2,1,0:T(8,128)(2,1)S(1)} %copy.233), kind=kOutput, calls=%fused_computation.174.clone.1 | convolution fusion | flops 307889280 | bytes 7353344 | tf_op jit(solution)/shard_map/while/body/eval_jaxpr/sub | solution.py:37
  284.2 5.6 %fusion.174 = (f32[8,128]{1,0:T(8,128)S(1)}, f32[8,128,1152]{2,1,0:T(8,128)}) fusion(bf16[8,1152,128]{2,1,0:T(8,128)(2,1)} %bitcast.361, pred[8,1152]{1,0:T(8,128)(4,1)S(1)} %broadcast_bitcast_fusion.2, bf16[1,8,128,128]{3,2,1,0:T(8,128)(2,1)S(1)} %copy.233), kind=kOutput, calls=%fused_computation.174.clone.1 | convolution fusion | flops 307889280 | bytes 7353344 | tf_op jit(solution)/shard_map/while/body/eval_jaxpr/sub | solution.py:37
  310.4 5.6 %fusion.174 = (f32[8,128]{1,0:T(8,128)S(1)}, f32[8,128,1152]{2,1,0:T(8,128)}) fusion(bf16[8,1152,128]{2,1,0:T(8,128)(2,1)} %bitcast.361, pred[8,1152]{1,0:T(8,128)(4,1)S(1)} %broadcast_bitcast_fusion.2, bf16[1,8,128,128]{3,2,1,0:T(8,128)(2,1)S(1)} %copy.233), kind=kOutput, calls=%fused_computation.174.clone.1 | convolution fusion | flops 307889280 | bytes 7353344 | tf_op jit(solution)/shard_map/while/body/eval_jaxpr/sub | solution.py:37
  336.5 5.6 %fusion.174 = (f32[8,128]{1,0:T(8,128)S(1)}, f32[8,128,1152]{2,1,0:T(8,128)}) fusion(bf16[8,1152,128]{2,1,0:T(8,128)(2,1)} %bitcast.361, pred[8,1152]{1,0:T(8,128)(4,1)S(1)} %broadcast_bitcast_fusion.2, bf16[1,8,128,128]{3,2,1,0:T(8,128)(2,1)S(1)} %copy.233), kind=kOutput, calls=%fused_computation.174.clone.1 | convolution fusion | flops 307889280 | bytes 7353344 | tf_op jit(solution)/shard_map/while/body/eval_jaxpr/sub | solution.py:37
  355.9 6.2 %convert.4 = bf16[6,2,16,128,128]{4,3,2,1,0:T(8,128)(2,1)S(1)} convert(f32[6,2,16,128,128]{4,3,2,1,0:T(8,128)} %get-tuple-element.300) | non-fusion elementwise | flops 3145728 | bytes 18874368 | tf_op jit(solution)/shard_map/convert.1
  370.6 6.3 %slice.576 = f32[6,2,8,128,128]{4,3,2,1,0:T(8,128)} slice(f32[6,2,16,128,128]{4,3,2,1,0:T(8,128)} %get-tuple-element.300), slice={[0:6], [0:2], [4:12], [0:128], [0:128]} | slice | bytes 12582912 | tf_op jit(solution)/shard_map/slice | solution.py:124
  386.3 15.4 %collective-permute-done.2 = bf16[6,2,4,128,128]{4,3,2,1,0:T(8,128)(2,1)} collective-permute-done((bf16[6,2,4,128,128]{4,3,2,1,0:T(8,128)(2,1)}, bf16[6,2,4,128,128]{4,3,2,1,0:T(8,128)(2,1)}, u32[]{:S(2)}, u32[]{:S(2)}) %collective-permute-start.2) | collective-permute-done | bytes 1572896 | tf_op jit(solution)/shard_map/ppermute | solution.py:27
  (354 shorter events, 224.2 us)
Async XLA Ops:
  7.3 8.9 %copy-start.12 = (s32[64,64]{1,0:T(8,128)S(1)}, s32[64,64]{1,0:T(8,128)}, u32[]{:S(2)}) copy-start(s32[64,64]{1,0:T(8,128)} %param.43) | copy-start | bytes 49156
  7.3 9.0 %copy-start.13 = (s32[64,9]{0,1:T(8,128)S(1)}, s32[64,9]{0,1:T(8,128)}, u32[]{:S(2)}) copy-start(s32[64,9]{0,1:T(8,128)} %param.38) | copy-start | bytes 6916
  7.3 9.1 %copy-start.10 = (bf16[1024,768]{1,0:T(8,128)(2,1)S(1)}, bf16[1024,768]{1,0:T(8,128)(2,1)}, u32[]{:S(2)}) copy-start(bf16[1024,768]{1,0:T(8,128)(2,1)} %param.34) | copy-start | bytes 4718596
  11.6 21.4 %collective-permute-start.4 = (bf16[4,8,16,768]{3,2,1,0:T(8,128)(2,1)}, bf16[4,8,16,768]{3,2,1,0:T(8,128)(2,1)}, u32[]{:S(2)}, u32[]{:S(2)}) collective-permute-start(bf16[4,8,16,768]{3,2,1,0:T(8,128)(2,1)} %get-tuple-element.414), channel_id=1, source_target_pairs={{0,28},{4,0},{8,4},{12,8},{16,12},{20,16},{24,20},{28,24},{1,29},{... | collective-permute-start | bytes 2359304 | tf_op jit(solution)/shard_map/ppermute | solution.py:146
  12.1 22.9 %collective-permute-start.5 = (bf16[4,8,16,768]{3,2,1,0:T(8,128)(2,1)}, bf16[4,8,16,768]{3,2,1,0:T(8,128)(2,1)}, u32[]{:S(2)}, u32[]{:S(2)}) collective-permute-start(bf16[4,8,16,768]{3,2,1,0:T(8,128)(2,1)} %get-tuple-element.413), channel_id=1, source_target_pairs={{0,24},{4,28},{8,0},{12,4},{16,8},{20,12},{24,16},{28,20},{1,25},{... | collective-permute-start | bytes 2359304 | tf_op jit(solution)/shard_map/ppermute | solution.py:146
  12.4 53.8 %collective-permute-start.6 = (bf16[4,8,16,768]{3,2,1,0:T(8,128)(2,1)}, bf16[4,8,16,768]{3,2,1,0:T(8,128)(2,1)}, u32[]{:S(2)}, u32[]{:S(2)}) collective-permute-start(bf16[4,8,16,768]{3,2,1,0:T(8,128)(2,1)} %get-tuple-element.412), channel_id=1, source_target_pairs={{0,20},{4,24},{8,28},{12,0},{16,4},{20,8},{24,12},{28,16},{1,21},{... | collective-permute-start | bytes 2359304 | tf_op jit(solution)/shard_map/ppermute | solution.py:146
  14.9 54.5 %collective-permute-start.7 = (bf16[4,8,16,768]{3,2,1,0:T(8,128)(2,1)}, bf16[4,8,16,768]{3,2,1,0:T(8,128)(2,1)}, u32[]{:S(2)}, u32[]{:S(2)}) collective-permute-start(bf16[4,8,16,768]{3,2,1,0:T(8,128)(2,1)} %get-tuple-element.411), channel_id=1, source_target_pairs={{0,16},{4,20},{8,24},{12,28},{16,0},{20,4},{24,8},{28,12},{1,17},{... | collective-permute-start | bytes 2359304 | tf_op jit(solution)/shard_map/ppermute | solution.py:146
  14.9 72.2 %collective-permute-start.8 = (bf16[4,8,16,768]{3,2,1,0:T(8,128)(2,1)}, bf16[4,8,16,768]{3,2,1,0:T(8,128)(2,1)}, u32[]{:S(2)}, u32[]{:S(2)}) collective-permute-start(bf16[4,8,16,768]{3,2,1,0:T(8,128)(2,1)} %get-tuple-element.410), channel_id=1, source_target_pairs={{0,12},{4,16},{8,20},{12,24},{16,28},{20,0},{24,4},{28,8},{1,13},{... | collective-permute-start | bytes 2359304 | tf_op jit(solution)/shard_map/ppermute | solution.py:146
  18.7 14.4 %copy-start.3 = (bf16[1024,768]{1,0:T(8,128)(2,1)S(1)}, bf16[1024,768]{1,0:T(8,128)(2,1)}, u32[]{:S(2)}) copy-start(bf16[1024,768]{1,0:T(8,128)(2,1)} %param.35) | copy-start | bytes 4718596
  18.7 14.4 %copy-start.4 = (bf16[1024,768]{1,0:T(8,128)(2,1)S(1)}, bf16[1024,768]{1,0:T(8,128)(2,1)}, u32[]{:S(2)}) copy-start(bf16[1024,768]{1,0:T(8,128)(2,1)} %param.36) | copy-start | bytes 4718596
  33.0 55.4 %collective-permute-start.9 = (bf16[4,8,16,768]{3,2,1,0:T(8,128)(2,1)}, bf16[4,8,16,768]{3,2,1,0:T(8,128)(2,1)S(1)}, u32[]{:S(2)}, u32[]{:S(2)}) collective-permute-start(bf16[4,8,16,768]{3,2,1,0:T(8,128)(2,1)} %get-tuple-element.409), channel_id=1, source_target_pairs={{0,8},{4,12},{8,16},{12,20},{16,24},{20,28},{24,0},{28,4},{1,9},{5... | collective-permute-start | bytes 2359304 | tf_op jit(solution)/shard_map/ppermute | solution.py:146
  35.0 53.4 %collective-permute-start.10 = (bf16[4,8,16,768]{3,2,1,0:T(8,128)(2,1)S(1)}, bf16[4,8,16,768]{3,2,1,0:T(8,128)(2,1)S(1)}, u32[]{:S(2)}, u32[]{:S(2)}) collective-permute-start(bf16[4,8,16,768]{3,2,1,0:T(8,128)(2,1)S(1)} %copy-done.11), channel_id=1, source_target_pairs={{0,4},{4,8},{8,12},{12,16},{16,20},{20,24},{24,28},{28,0},{1,5},{5... | collective-permute-start | bytes 2359304 | tf_op jit(solution)/shard_map/ppermute | solution.py:146
  66.2 110.8 %collective-permute-start.1 = (bf16[2,512,768]{2,1,0:T(8,128)(2,1)}, bf16[2,512,768]{2,1,0:T(8,128)(2,1)}, u32[]{:S(2)}, u32[]{:S(2)}) collective-permute-start(bf16[2,512,768]{2,1,0:T(8,128)(2,1)} %get-tuple-element.420), channel_id=1, source_target_pairs={{4,0},{8,4},{12,8},{16,12},{20,16},{24,20},{28,24},{5,1},{9,5},{13... | collective-permute-start | bytes 4718600 | tf_op jit(solution)/shard_map/ppermute | solution.py:19
  69.3 107.7 %collective-permute-start = (bf16[2,512,768]{2,1,0:T(8,128)(2,1)}, bf16[2,512,768]{2,1,0:T(8,128)(2,1)}, u32[]{:S(2)}, u32[]{:S(2)}) collective-permute-start(bf16[2,512,768]{2,1,0:T(8,128)(2,1)} %get-tuple-element.419), channel_id=1, source_target_pairs={{0,4},{4,8},{8,12},{12,16},{16,20},{20,24},{24,28},{1,5},{5,9},{9,... | collective-permute-start | bytes 4718600 | tf_op jit(solution)/shard_map/ppermute | solution.py:18
  170.8 241.6 %all-to-all-start = ((bf16[4,64,16,768]{3,2,0,1:T(8,128)(2,1)}), bf16[4,64,16,768]{3,2,0,1:T(8,128)(2,1)}, u32[]{:S(2)}, u32[]{:S(2)}) async-start(bf16[4,64,16,768]{3,2,0,1:T(8,128)(2,1)} %copy.169), calls=%async_computation | async-start | bytes 12582912 | tf_op jit(solution)/shard_map/all_to_all | solution.py:162
  211.5 4.8 %slice-start.1 = ((s8[4718592]{0:T(1024)(128)(4,1)}), s8[524288]{0:T(1024)(128)(4,1)S(1)}, s32[]{:S(2)}) async-start(s8[4718592]{0:T(1024)(128)(4,1)} %bitcast.359), calls=%async_computation.2 | async-start | bytes 1048576 | tf_op jit(solution)/shard_map/while
  237.6 4.8 %slice-start.1 = ((s8[4718592]{0:T(1024)(128)(4,1)}), s8[524288]{0:T(1024)(128)(4,1)S(1)}, s32[]{:S(2)}) async-start(s8[4718592]{0:T(1024)(128)(4,1)} %bitcast.359), calls=%async_computation.2 | async-start | bytes 1048576 | tf_op jit(solution)/shard_map/while
  263.7 4.8 %slice-start.1 = ((s8[4718592]{0:T(1024)(128)(4,1)}), s8[524288]{0:T(1024)(128)(4,1)S(1)}, s32[]{:S(2)}) async-start(s8[4718592]{0:T(1024)(128)(4,1)} %bitcast.359), calls=%async_computation.2 | async-start | bytes 1048576 | tf_op jit(solution)/shard_map/while
  289.8 4.8 %slice-start.1 = ((s8[4718592]{0:T(1024)(128)(4,1)}), s8[524288]{0:T(1024)(128)(4,1)S(1)}, s32[]{:S(2)}) async-start(s8[4718592]{0:T(1024)(128)(4,1)} %bitcast.359), calls=%async_computation.2 | async-start | bytes 1048576 | tf_op jit(solution)/shard_map/while
  342.2 4.8 %slice-start.1 = ((s8[4718592]{0:T(1024)(128)(4,1)}), s8[524288]{0:T(1024)(128)(4,1)S(1)}, s32[]{:S(2)}) async-start(s8[4718592]{0:T(1024)(128)(4,1)} %bitcast.359), calls=%async_computation.2 | async-start | bytes 1048576 | tf_op jit(solution)/shard_map/while
  364.0 37.7 %collective-permute-start.2 = (bf16[6,2,4,128,128]{4,3,2,1,0:T(8,128)(2,1)}, bf16[6,2,4,128,128]{4,3,2,1,0:T(8,128)(2,1)}, u32[]{:S(2)}, u32[]{:S(2)}) collective-permute-start(bf16[6,2,4,128,128]{4,3,2,1,0:T(8,128)(2,1)} %get-tuple-element.416), channel_id=1, source_target_pairs={{4,0},{8,4},{12,8},{16,12},{20,16},{24,20},{28,24},{5,1},{9,5},{13... | collective-permute-start | bytes 4718600 | tf_op jit(solution)/shard_map/ppermute | solution.py:27
  366.3 10.6 %copy-start.7 = (bf16[6,8,128,128]{3,2,1,0:T(8,128)(2,1)S(1)}, bf16[6,8,128,128]{3,2,1,0:T(8,128)(2,1)}, u32[]{:S(2)}) copy-start(bf16[6,8,128,128]{3,2,1,0:T(8,128)(2,1)} %get-tuple-element.299) | copy-start | bytes 4718596
  366.3 38.2 %collective-permute-start.3 = (bf16[6,2,4,128,128]{4,3,2,1,0:T(8,128)(2,1)}, bf16[6,2,4,128,128]{4,3,2,1,0:T(8,128)(2,1)}, u32[]{:S(2)}, u32[]{:S(2)}) collective-permute-start(bf16[6,2,4,128,128]{4,3,2,1,0:T(8,128)(2,1)} %get-tuple-element.415), channel_id=1, source_target_pairs={{0,4},{4,8},{8,12},{12,16},{16,20},{20,24},{24,28},{1,5},{5,9},{9,... | collective-permute-start | bytes 4718600 | tf_op jit(solution)/shard_map/ppermute | solution.py:27
  381.9 19.7 %copy-start.1 = (f32[6,2,8,128,128]{4,3,2,1,0:T(8,128)S(1)}, f32[6,2,8,128,128]{4,3,2,1,0:T(8,128)}, u32[]{:S(2)}) copy-start(f32[6,2,8,128,128]{4,3,2,1,0:T(8,128)} %slice.576) | copy-start | bytes 18874372
  (20 other events, 63.9 us)
